TPU v7x, 256 devices: a whole 4x4x8 slice. The times are simulated.
256 devices in a mesh: chan: 32 (over y_lo, z, core), tm: 8 (over y_hi, x).
Axes of the slice: x: 4, y: 4 (y_hi: 2, y_lo: 2; y = y_hi * 2 + y_lo), z: 8, core: 2. Of those that a mesh axis runs over, the one named last changes fastest.
Arguments:
- traces: bfloat16 [256, 6144], P('chan', 'tm'), may hold values from -6 to 6
- validity: int32 [256], P('chan'), may hold values 0 or 1
- owners: int32 [8], replicated, may hold values from 0 to 31
Outputs:
- correlations: float32 [8, 256, 8, 2048], P(None, 'chan', None, 'tm')
All inputs are finite; a program needn't handle non-finite values. No bound on the sum of `validity` on one device may be relied on, other than what follows from the above.
Results may differ from a plain program's by a relative error of at most 0.0003.
Values may be sent and summed in bfloat16 or wider, within the bound.
No kernel may reach another device: no remote copies, remote signals or barrier semaphores. Data moves between devices by JAX's collectives and lax.ppermute only.
A program may use at most 64 MiB of HBM per device.

v0:
```python
import math
import jax
import jax.numpy as jnp
from jax import lax
from jax.sharding import PartitionSpec as P

LAG = 1024


def broadcast(block, axis, holder):
    block = jnp.where(lax.axis_index(axis) == holder, block, jnp.zeros_like(block))
    return lax.psum(block, axis)


def toeplitz(segment, lag_rows, time_cols):
    seg_width = segment.shape[1]
    repeated = jnp.tile(segment, (1, lag_rows + 1))[:, : lag_rows * (seg_width + 1)]
    return repeated.reshape(segment.shape[0], lag_rows, seg_width + 1)[:, :, :time_cols]


def on_device(traces, validity, owners):
    channels_here = traces.shape[0]
    step_count = owners.shape[0]
    receiver = lax.all_gather(traces, "tm", axis=1, tiled=True)
    time_len = receiver.shape[1]
    lag_dev = 2 * LAG // lax.axis_size("tm")
    valid_flags = validity.astype(jnp.bfloat16)

    def fetch_piece(step_number, buffers):
        source_pieces, source_flags = buffers
        fetched, fetched_flags = (
            broadcast(traces, "chan", owners[step_number]),
            broadcast(valid_flags, "chan", owners[step_number]),
        )
        return (
            source_pieces.at[step_number].set(fetched),
            source_flags.at[step_number].set(fetched_flags),
        )

    initial = (
        jnp.zeros((step_count,) + traces.shape, jnp.bfloat16),
        jnp.zeros((step_count, channels_here), jnp.bfloat16),
    )
    source_pieces, source_flags = lax.fori_loop(0, step_count, fetch_piece, initial)
    sources = lax.all_gather(source_pieces, "tm", axis=2, tiled=True)
    padded = jnp.pad(receiver, ((0, 0), (LAG, LAG)))
    offset = lax.axis_index("tm") * lag_dev
    block_len = 512

    def accumulate(block_number, summed):
        begin_at = block_number * block_len
        segment = lax.dynamic_slice_in_dim(padded, begin_at + offset, block_len + lag_dev, 1)
        shifted = toeplitz(segment, lag_dev, block_len)
        source_block = lax.dynamic_slice_in_dim(sources, begin_at, block_len, 2)
        return summed + jnp.einsum(
            "rku,scu->srck", shifted, source_block, preferred_element_type=jnp.float32
        )

    zeros_acc = jnp.zeros((step_count, channels_here, channels_here, lag_dev), jnp.float32)
    summed = lax.fori_loop(0, time_len // block_len, accumulate, zeros_acc)
    pair_weight = (
        validity.astype(jnp.float32)[None, :, None, None]
        * source_flags.astype(jnp.float32)[:, None, :, None]
    )
    return summed * (1.0 / math.sqrt(time_len)) * pair_weight


def solution(mesh):
    placed = (P("chan", "tm"), P("chan"), P())
    return jax.shard_map(
        on_device,
        mesh=mesh,
        in_specs=placed,
        out_specs=P(None, "chan", None, "tm"),
        check_vma=False,
    )
```

profile of v0, /device:TPU:6, one launch (start us, length us, event | category | flops | bytes accessed | tf_op | source)
XLA Modules:
  0.0 1211.4 jit_solution(13575276252941144519)
XLA Ops:
  0.8 891.6 %while.31 = (s32[]{:T(128)}, bf16[8,8,768]{2,1,0:T(8,128)(2,1)S(1)}, bf16[8,8]{1,0:T(8,128)(2,1)S(1)}, s32[8]{0:T(128)}, bf16[8,768]{1,0:T(8,128)(2,1)}, /*index...) while((s32[]{:T(128)}, ...), condition=%wide.region_5.6_spmd, body=%wide.region_0.5_spmd.sunk | while | flops 18488 | bytes 86400 | solution.py:44
  2.7 110.7 %all-reduce.3 = (bf16[1,8,768]{2,1,0:T(8,128)(2,1)S(1)}, bf16[1,8]{1,0:T(2,128)(2,1)S(1)}) all-reduce(bf16[1,8,768]{2,1,0:T(8,128)(2,1)S(1)} %select_bitcast_fusion.2, bf16[1,8]{1,0:T(2,128)(2,1)S(1)} %fusion.11), channel_id=1, replica_groups=mesh['chan'=32,'tm'=8] {'chan'}, use_global_device_ids=true, to_apply=%region_2.2 | all-reduce | flops 6152 | bytes 24608 | tf_op jit(solution)/shard_map/while/body/eval_jaxpr/psum | solution.py:12
  113.5 1.4 and_reduce_fusion.4
  115.5 1.4 and_reduce_fusion.5
  119.6 104.5 %all-reduce.3 = (bf16[1,8,768]{2,1,0:T(8,128)(2,1)S(1)}, bf16[1,8]{1,0:T(2,128)(2,1)S(1)}) all-reduce(bf16[1,8,768]{2,1,0:T(8,128)(2,1)S(1)} %select_bitcast_fusion.2, bf16[1,8]{1,0:T(2,128)(2,1)S(1)} %fusion.11), channel_id=1, replica_groups=mesh['chan'=32,'tm'=8] {'chan'}, use_global_device_ids=true, to_apply=%region_2.2 | all-reduce | flops 6152 | bytes 24608 | tf_op jit(solution)/shard_map/while/body/eval_jaxpr/psum | solution.py:12
  224.0 1.4 and_reduce_fusion.4
  226.1 1.4 and_reduce_fusion.5
  230.8 104.5 %all-reduce.3 = (bf16[1,8,768]{2,1,0:T(8,128)(2,1)S(1)}, bf16[1,8]{1,0:T(2,128)(2,1)S(1)}) all-reduce(bf16[1,8,768]{2,1,0:T(8,128)(2,1)S(1)} %select_bitcast_fusion.2, bf16[1,8]{1,0:T(2,128)(2,1)S(1)} %fusion.11), channel_id=1, replica_groups=mesh['chan'=32,'tm'=8] {'chan'}, use_global_device_ids=true, to_apply=%region_2.2 | all-reduce | flops 6152 | bytes 24608 | tf_op jit(solution)/shard_map/while/body/eval_jaxpr/psum | solution.py:12
  335.3 1.4 and_reduce_fusion.4
  337.3 1.4 and_reduce_fusion.5
  341.4 104.6 %all-reduce.3 = (bf16[1,8,768]{2,1,0:T(8,128)(2,1)S(1)}, bf16[1,8]{1,0:T(2,128)(2,1)S(1)}) all-reduce(bf16[1,8,768]{2,1,0:T(8,128)(2,1)S(1)} %select_bitcast_fusion.2, bf16[1,8]{1,0:T(2,128)(2,1)S(1)} %fusion.11), channel_id=1, replica_groups=mesh['chan'=32,'tm'=8] {'chan'}, use_global_device_ids=true, to_apply=%region_2.2 | all-reduce | flops 6152 | bytes 24608 | tf_op jit(solution)/shard_map/while/body/eval_jaxpr/psum | solution.py:12
  446.0 1.4 and_reduce_fusion.4
  448.0 1.4 and_reduce_fusion.5
  452.0 104.5 %all-reduce.3 = (bf16[1,8,768]{2,1,0:T(8,128)(2,1)S(1)}, bf16[1,8]{1,0:T(2,128)(2,1)S(1)}) all-reduce(bf16[1,8,768]{2,1,0:T(8,128)(2,1)S(1)} %select_bitcast_fusion.2, bf16[1,8]{1,0:T(2,128)(2,1)S(1)} %fusion.11), channel_id=1, replica_groups=mesh['chan'=32,'tm'=8] {'chan'}, use_global_device_ids=true, to_apply=%region_2.2 | all-reduce | flops 6152 | bytes 24608 | tf_op jit(solution)/shard_map/while/body/eval_jaxpr/psum | solution.py:12
  558.6 1.4 and_reduce_fusion.5
  562.6 104.5 %all-reduce.3 = (bf16[1,8,768]{2,1,0:T(8,128)(2,1)S(1)}, bf16[1,8]{1,0:T(2,128)(2,1)S(1)}) all-reduce(bf16[1,8,768]{2,1,0:T(8,128)(2,1)S(1)} %select_bitcast_fusion.2, bf16[1,8]{1,0:T(2,128)(2,1)S(1)} %fusion.11), channel_id=1, replica_groups=mesh['chan'=32,'tm'=8] {'chan'}, use_global_device_ids=true, to_apply=%region_2.2 | all-reduce | flops 6152 | bytes 24608 | tf_op jit(solution)/shard_map/while/body/eval_jaxpr/psum | solution.py:12
  667.1 1.4 and_reduce_fusion.4
  669.1 1.4 and_reduce_fusion.5
  673.2 104.5 %all-reduce.3 = (bf16[1,8,768]{2,1,0:T(8,128)(2,1)S(1)}, bf16[1,8]{1,0:T(2,128)(2,1)S(1)}) all-reduce(bf16[1,8,768]{2,1,0:T(8,128)(2,1)S(1)} %select_bitcast_fusion.2, bf16[1,8]{1,0:T(2,128)(2,1)S(1)} %fusion.11), channel_id=1, replica_groups=mesh['chan'=32,'tm'=8] {'chan'}, use_global_device_ids=true, to_apply=%region_2.2 | all-reduce | flops 6152 | bytes 24608 | tf_op jit(solution)/shard_map/while/body/eval_jaxpr/psum | solution.py:12
  777.6 1.4 and_reduce_fusion.4
  779.7 1.4 and_reduce_fusion.5
  783.7 104.5 %all-reduce.3 = (bf16[1,8,768]{2,1,0:T(8,128)(2,1)S(1)}, bf16[1,8]{1,0:T(2,128)(2,1)S(1)}) all-reduce(bf16[1,8,768]{2,1,0:T(8,128)(2,1)S(1)} %select_bitcast_fusion.2, bf16[1,8]{1,0:T(2,128)(2,1)S(1)} %fusion.11), channel_id=1, replica_groups=mesh['chan'=32,'tm'=8] {'chan'}, use_global_device_ids=true, to_apply=%region_2.2 | all-reduce | flops 6152 | bytes 24608 | tf_op jit(solution)/shard_map/while/body/eval_jaxpr/psum | solution.py:12
  888.2 1.4 and_reduce_fusion.4
  890.2 1.4 and_reduce_fusion.5
  892.3 37.7 %all_gather.6 = bf16[8,8,6144]{2,1,0:T(8,128)(2,1)} all-gather(bf16[8,8,768]{2,1,0:T(8,128)(2,1)S(1)} %get-tuple-element.253), channel_id=1, replica_groups=mesh['chan'=32,'tm'=8] {'tm'}, dimensions={2}, use_global_device_ids=true | all-gather | bytes 884736 | tf_op jit(solution)/shard_map/all_gather | solution.py:45
  930.1 34.4 %all_gather.7 = bf16[8,6144]{1,0:T(8,128)(2,1)S(1)} all-gather(bf16[8,768]{1,0:T(8,128)(2,1)} %get-tuple-element.441), channel_id=1, replica_groups=mesh['chan'=32,'tm'=8] {'tm'}, dimensions={1}, use_global_device_ids=true | all-gather | bytes 110592 | tf_op jit(solution)/shard_map/all_gather | solution.py:24
  964.5 244.9 %while.32 = (s32[]{:T(128)}, f32[8,8,8,256]{3,2,1,0:T(8,128)}, bf16[8,8,6144]{2,1,0:T(8,128)(2,1)}, s32[]{:T(128)}, bf16[8,8192]{1,0:T(8,128)(2,1)S(1)}, /*index...) while((s32[]{:T(128)}, f32[8,8,8,256]{3,2,1,0:T(8,128)}, ...), condition=%wide.region_7.8_spmd.clone, body=%wide.region_6.7_spmd.clone.sunk | while | flops 134479888 | bytes 29499664 | solution.py:60
  965.0 6.4 reshape.130
  971.4 10.3 reshape.131
  981.7 2.5 fusion.13
  985.4 6.4 reshape.130
  991.8 10.3 reshape.131
  1002.1 2.5 fusion.13
  1005.8 6.4 reshape.130
  1012.2 10.3 reshape.131
  1022.5 2.5 fusion.13
  1026.2 6.4 reshape.130
  1032.6 10.3 reshape.131
  1042.9 2.5 fusion.13
  1046.6 6.4 reshape.130
  1053.0 10.3 reshape.131
  1063.3 2.5 fusion.13
  1067.0 6.4 reshape.130
  1073.4 10.3 reshape.131
  1083.7 2.5 fusion.13
  1087.4 6.4 reshape.130
  1093.8 10.3 reshape.131
  1104.1 2.5 fusion.13
  1107.8 6.4 reshape.130
  1114.2 10.3 reshape.131
  1124.5 2.5 fusion.13
  1128.2 6.4 reshape.130
  1134.6 10.3 reshape.131
  1144.9 2.5 fusion.13
  1148.7 6.4 reshape.130
  1155.0 10.3 reshape.131
  1165.3 2.5 fusion.13
  1169.1 6.4 reshape.130
  1175.4 10.3 reshape.131
  1185.7 2.5 fusion.13
  1189.5 6.4 reshape.130
  1195.8 10.3 reshape.131
  1206.1 2.5 fusion.13
  1209.5 2.0 broadcast_multiply_fusion
  (140 shorter events, 38.9 us)
Async XLA Ops:
  971.4 10.3 copy-start
  984.1 0.8 copy-start.1
  991.8 10.3 copy-start
  1004.5 0.8 copy-start.1
  1012.2 10.3 copy-start
  1025.0 0.8 copy-start.1
  1032.6 10.3 copy-start
  1045.4 0.8 copy-start.1
  1053.0 10.3 copy-start
  1065.8 0.8 copy-start.1
  1073.4 10.3 copy-start
  1086.2 0.8 copy-start.1
  1093.8 10.3 copy-start
  1106.6 0.8 copy-start.1
  1114.2 10.3 copy-start
  1127.0 0.8 copy-start.1
  1134.6 10.3 copy-start
  1147.4 0.8 copy-start.1
  1155.0 10.3 copy-start
  1167.8 0.8 copy-start.1
  1175.4 10.3 copy-start
  1188.2 0.8 copy-start.1
  1195.8 10.3 copy-start
  1208.6 0.8 copy-start.1
where the time goes:
time: 1210 us
  blocking collectives  914 us (76%)
  local copies, waits for them, and re-layouts  226 us (19%)
  other arithmetic  36.3 us (3%)
  matrix products  29.5 us (2%)
    psum x8, blocking collectives, broadcast(): return lax.psum(block, axis)  842 us
    reshape x12, local copies, waits for them, and re-layouts, toeplitz(): repeated.reshape(segment.shape[0], lag_rows, seg_width + 1)  123 us
    while x60, local copies, waits for them, and re-layouts  86 us
    all_gather x1, blocking collectives, on_device(): sources = lax.all_gather(source_pieces, 'tm', axis=2, tiled=True)  37.7 us
    all_gather x1, blocking collectives, on_device(): receiver = lax.all_gather(traces, 'tm', axis=1, tiled=True)  34.4 us
    dot_general x12, matrix products, accumulate(): jnp.einsum('rku,scu->srck', shifted, source_block, preferred_element_type...  29.5 us
    another operation x40, other arithmetic  28.3 us

commit v1 on v0

--- a/solution.py
+++ b/solution.py
@@ -9,7 +9,7 @@
 
 def broadcast(block, axis, holder):
     block = jnp.where(lax.axis_index(axis) == holder, block, jnp.zeros_like(block))
-    return lax.psum(block, axis)
+    return jnp.sum(lax.all_gather(block, axis), axis=0)
 
 
 def toeplitz(segment, lag_rows, time_cols):

time: 1210 us -> 1080 us (0.89)
  blocking collectives: 914 us -> 769 us
  local copies, waits for them, and re-layouts: 226 us -> 239 us
    psum x8 -> x0, blocking collectives: 842 us -> none  [broadcast(): return lax.psum(block, axis)]
    while x0 -> x8, blocking collectives: none -> 438 us
    all_gather x0 -> x8, blocking collectives: none -> 258 us  [broadcast(): return jnp.sum(lax.all_gather(block, axis), axis=0)]
    while x60 -> x84, local copies, waits for them, and re-layouts: 86 us -> 98.5 us
    another operation x40 -> x24, other arithmetic: 28.3 us -> 26.4 us
where the time goes in v1:
time: 1080 us
  blocking collectives  769 us (71%)
  local copies, waits for them, and re-layouts  239 us (22%)
  other arithmetic  35.4 us (3%)
  matrix products  29.5 us (3%)
    while x8, blocking collectives  438 us
    all_gather x8, blocking collectives, broadcast(): return jnp.sum(lax.all_gather(block, axis), axis=0)  258 us
    reshape x12, local copies, waits for them, and re-layouts, toeplitz(): repeated.reshape(segment.shape[0], lag_rows, seg_width + 1)  123 us
    while x84, local copies, waits for them, and re-layouts  98.5 us
    all_gather x1, blocking collectives, on_device(): sources = lax.all_gather(source_pieces, 'tm', axis=2, tiled=True)  37.8 us
    all_gather x1, blocking collectives, on_device(): receiver = lax.all_gather(traces, 'tm', axis=1, tiled=True)  34.4 us
    dot_general x12, matrix products, accumulate(): jnp.einsum('rku,scu->srck', shifted, source_block, preferred_element_type...  29.5 us
    another operation x24, other arithmetic  26.4 us

profile of v1, /device:TPU:6, one launch (start us, length us, event | category | flops | bytes accessed | tf_op | source)
XLA Modules:
  0.0 1082.6 jit_solution(10219744990861748185)
XLA Ops:
  0.8 762.7 %while.34 = (s32[]{:T(128)}, bf16[8,8,768]{2,1,0:T(8,128)(2,1)S(1)}, bf16[8,8]{1,0:T(8,128)(2,1)S(1)}, s32[8]{0:T(128)}, bf16[8,768]{1,0:T(8,128)(2,1)}, /*index...) while((s32[]{:T(128)}, ...), condition=%wide.region_5.6_spmd, body=%wide.region_0.5_spmd.sunk | while | flops 203307 | bytes 876008 | solution.py:44
  2.6 38.3 %all-gather.3 = bf16[256,768]{1,0:T(8,128)(2,1)S(1)} all-gather(bf16[8,768]{1,0:T(8,128)(2,1)S(1)} %broadcast_select_fusion.6), channel_id=2, replica_groups=mesh['chan'=32,'tm'=8] {'chan'}, dimensions={0}, use_global_device_ids=true | all-gather | bytes 405504 | tf_op jit(solution)/shard_map/while/body/eval_jaxpr/all_gather | solution.py:12
  42.9 1.4 and_reduce_fusion.5
  46.5 53.4 %all-reduce.3 = bf16[256]{0:T(256)(128)(2,1)S(1)} all-reduce(bf16[256]{0:T(256)(128)(2,1)S(1)} %dynamic-update-slice.24), channel_id=3, replica_groups=mesh['chan'=32,'tm'=8] {'chan'}, use_global_device_ids=true, to_apply=%add.1 | all-reduce | flops 256 | bytes 1024 | tf_op jit(solution)/shard_map/while
  102.4 31.5 %all-gather.3 = bf16[256,768]{1,0:T(8,128)(2,1)S(1)} all-gather(bf16[8,768]{1,0:T(8,128)(2,1)S(1)} %broadcast_select_fusion.6), channel_id=2, replica_groups=mesh['chan'=32,'tm'=8] {'chan'}, dimensions={0}, use_global_device_ids=true | all-gather | bytes 405504 | tf_op jit(solution)/shard_map/while/body/eval_jaxpr/all_gather | solution.py:12
  135.9 1.4 and_reduce_fusion.5
  139.5 55.0 %all-reduce.3 = bf16[256]{0:T(256)(128)(2,1)S(1)} all-reduce(bf16[256]{0:T(256)(128)(2,1)S(1)} %dynamic-update-slice.24), channel_id=3, replica_groups=mesh['chan'=32,'tm'=8] {'chan'}, use_global_device_ids=true, to_apply=%add.1 | all-reduce | flops 256 | bytes 1024 | tf_op jit(solution)/shard_map/while
  197.7 31.4 %all-gather.3 = bf16[256,768]{1,0:T(8,128)(2,1)S(1)} all-gather(bf16[8,768]{1,0:T(8,128)(2,1)S(1)} %broadcast_select_fusion.6), channel_id=2, replica_groups=mesh['chan'=32,'tm'=8] {'chan'}, dimensions={0}, use_global_device_ids=true | all-gather | bytes 405504 | tf_op jit(solution)/shard_map/while/body/eval_jaxpr/all_gather | solution.py:12
  231.2 1.4 and_reduce_fusion.5
  234.8 55.0 %all-reduce.3 = bf16[256]{0:T(256)(128)(2,1)S(1)} all-reduce(bf16[256]{0:T(256)(128)(2,1)S(1)} %dynamic-update-slice.24), channel_id=3, replica_groups=mesh['chan'=32,'tm'=8] {'chan'}, use_global_device_ids=true, to_apply=%add.1 | all-reduce | flops 256 | bytes 1024 | tf_op jit(solution)/shard_map/while
  292.3 31.5 %all-gather.3 = bf16[256,768]{1,0:T(8,128)(2,1)S(1)} all-gather(bf16[8,768]{1,0:T(8,128)(2,1)S(1)} %broadcast_select_fusion.6), channel_id=2, replica_groups=mesh['chan'=32,'tm'=8] {'chan'}, dimensions={0}, use_global_device_ids=true | all-gather | bytes 405504 | tf_op jit(solution)/shard_map/while/body/eval_jaxpr/all_gather | solution.py:12
  325.8 1.4 and_reduce_fusion.5
  329.3 55.0 %all-reduce.3 = bf16[256]{0:T(256)(128)(2,1)S(1)} all-reduce(bf16[256]{0:T(256)(128)(2,1)S(1)} %dynamic-update-slice.24), channel_id=3, replica_groups=mesh['chan'=32,'tm'=8] {'chan'}, use_global_device_ids=true, to_apply=%add.1 | all-reduce | flops 256 | bytes 1024 | tf_op jit(solution)/shard_map/while
  386.9 31.5 %all-gather.3 = bf16[256,768]{1,0:T(8,128)(2,1)S(1)} all-gather(bf16[8,768]{1,0:T(8,128)(2,1)S(1)} %broadcast_select_fusion.6), channel_id=2, replica_groups=mesh['chan'=32,'tm'=8] {'chan'}, dimensions={0}, use_global_device_ids=true | all-gather | bytes 405504 | tf_op jit(solution)/shard_map/while/body/eval_jaxpr/all_gather | solution.py:12
  420.4 1.4 and_reduce_fusion.5
  423.9 55.0 %all-reduce.3 = bf16[256]{0:T(256)(128)(2,1)S(1)} all-reduce(bf16[256]{0:T(256)(128)(2,1)S(1)} %dynamic-update-slice.24), channel_id=3, replica_groups=mesh['chan'=32,'tm'=8] {'chan'}, use_global_device_ids=true, to_apply=%add.1 | all-reduce | flops 256 | bytes 1024 | tf_op jit(solution)/shard_map/while
  481.5 31.5 %all-gather.3 = bf16[256,768]{1,0:T(8,128)(2,1)S(1)} all-gather(bf16[8,768]{1,0:T(8,128)(2,1)S(1)} %broadcast_select_fusion.6), channel_id=2, replica_groups=mesh['chan'=32,'tm'=8] {'chan'}, dimensions={0}, use_global_device_ids=true | all-gather | bytes 405504 | tf_op jit(solution)/shard_map/while/body/eval_jaxpr/all_gather | solution.py:12
  514.9 1.4 and_reduce_fusion.5
  518.5 55.0 %all-reduce.3 = bf16[256]{0:T(256)(128)(2,1)S(1)} all-reduce(bf16[256]{0:T(256)(128)(2,1)S(1)} %dynamic-update-slice.24), channel_id=3, replica_groups=mesh['chan'=32,'tm'=8] {'chan'}, use_global_device_ids=true, to_apply=%add.1 | all-reduce | flops 256 | bytes 1024 | tf_op jit(solution)/shard_map/while
  576.1 31.5 %all-gather.3 = bf16[256,768]{1,0:T(8,128)(2,1)S(1)} all-gather(bf16[8,768]{1,0:T(8,128)(2,1)S(1)} %broadcast_select_fusion.6), channel_id=2, replica_groups=mesh['chan'=32,'tm'=8] {'chan'}, dimensions={0}, use_global_device_ids=true | all-gather | bytes 405504 | tf_op jit(solution)/shard_map/while/body/eval_jaxpr/all_gather | solution.py:12
  609.5 1.4 and_reduce_fusion.5
  613.1 55.0 %all-reduce.3 = bf16[256]{0:T(256)(128)(2,1)S(1)} all-reduce(bf16[256]{0:T(256)(128)(2,1)S(1)} %dynamic-update-slice.24), channel_id=3, replica_groups=mesh['chan'=32,'tm'=8] {'chan'}, use_global_device_ids=true, to_apply=%add.1 | all-reduce | flops 256 | bytes 1024 | tf_op jit(solution)/shard_map/while
  670.7 31.5 %all-gather.3 = bf16[256,768]{1,0:T(8,128)(2,1)S(1)} all-gather(bf16[8,768]{1,0:T(8,128)(2,1)S(1)} %broadcast_select_fusion.6), channel_id=2, replica_groups=mesh['chan'=32,'tm'=8] {'chan'}, dimensions={0}, use_global_device_ids=true | all-gather | bytes 405504 | tf_op jit(solution)/shard_map/while/body/eval_jaxpr/all_gather | solution.py:12
  707.7 55.0 %all-reduce.3 = bf16[256]{0:T(256)(128)(2,1)S(1)} all-reduce(bf16[256]{0:T(256)(128)(2,1)S(1)} %dynamic-update-slice.24), channel_id=3, replica_groups=mesh['chan'=32,'tm'=8] {'chan'}, use_global_device_ids=true, to_apply=%add.1 | all-reduce | flops 256 | bytes 1024 | tf_op jit(solution)/shard_map/while
  763.4 37.8 %all_gather.34 = bf16[8,8,6144]{2,1,0:T(8,128)(2,1)} all-gather(bf16[8,8,768]{2,1,0:T(8,128)(2,1)S(1)} %get-tuple-element.316), channel_id=1, replica_groups=mesh['chan'=32,'tm'=8] {'tm'}, dimensions={2}, use_global_device_ids=true | all-gather | bytes 884736 | tf_op jit(solution)/shard_map/all_gather | solution.py:45
  801.2 34.4 %all_gather.35 = bf16[8,6144]{1,0:T(8,128)(2,1)S(1)} all-gather(bf16[8,768]{1,0:T(8,128)(2,1)} %get-tuple-element.510), channel_id=1, replica_groups=mesh['chan'=32,'tm'=8] {'tm'}, dimensions={1}, use_global_device_ids=true | all-gather | bytes 110592 | tf_op jit(solution)/shard_map/all_gather | solution.py:24
  835.6 244.9 %while.35 = (s32[]{:T(128)}, f32[8,8,8,256]{3,2,1,0:T(8,128)}, bf16[8,8,6144]{2,1,0:T(8,128)(2,1)}, s32[]{:T(128)}, bf16[8,8192]{1,0:T(8,128)(2,1)S(1)}, /*index...) while((s32[]{:T(128)}, f32[8,8,8,256]{3,2,1,0:T(8,128)}, ...), condition=%wide.region_7.8_spmd.clone, body=%wide.region_6.7_spmd.clone.sunk | while | flops 134479888 | bytes 29499664 | solution.py:60
  836.1 6.4 reshape.183
  842.5 10.3 reshape.184
  852.8 2.5 fusion.13
  856.6 6.4 reshape.183
  862.9 10.3 reshape.184
  873.2 2.5 fusion.13
  877.0 6.4 reshape.183
  883.3 10.3 reshape.184
  893.6 2.5 fusion.13
  897.4 6.4 reshape.183
  903.7 10.3 reshape.184
  914.0 2.5 fusion.13
  917.8 6.4 reshape.183
  924.1 10.3 reshape.184
  934.4 2.5 fusion.13
  938.2 6.4 reshape.183
  944.5 10.3 reshape.184
  954.8 2.5 fusion.13
  958.6 6.4 reshape.183
  964.9 10.3 reshape.184
  975.2 2.5 fusion.13
  979.0 6.4 reshape.183
  985.4 10.3 reshape.184
  995.6 2.5 fusion.13
  999.4 6.4 reshape.183
  1005.8 10.3 reshape.184
  1016.0 2.5 fusion.13
  1019.8 6.4 reshape.183
  1026.2 10.3 reshape.184
  1036.5 2.5 fusion.13
  1040.2 6.4 reshape.183
  1046.6 10.3 reshape.184
  1056.9 2.5 fusion.13
  1060.6 6.4 reshape.183
  1067.0 10.3 reshape.184
  1077.3 2.5 fusion.13
  1080.6 2.0 broadcast_multiply_fusion
  (196 shorter events, 62.4 us)
Async XLA Ops:
  842.5 10.3 copy-start
  855.3 0.8 copy-start.1
  862.9 10.3 copy-start
  875.7 0.8 copy-start.1
  883.3 10.3 copy-start
  896.1 0.8 copy-start.1
  903.7 10.3 copy-start
  916.5 0.8 copy-start.1
  924.1 10.3 copy-start
  936.9 0.8 copy-start.1
  944.5 10.3 copy-start
  957.3 0.8 copy-start.1
  964.9 10.3 copy-start
  977.7 0.8 copy-start.1
  985.3 10.3 copy-start
  998.1 0.8 copy-start.1
  1005.8 10.3 copy-start
  1018.5 0.8 copy-start.1
  1026.2 10.3 copy-start
  1038.9 0.8 copy-start.1
  1046.6 10.3 copy-start
  1059.3 0.8 copy-start.1
  1067.0 10.3 copy-start
  1079.7 0.8 copy-start.1
